TPU v7x, 256 devices: a whole 4x4x8 slice. The times are simulated.
256 devices in a mesh: mem: 64 (over z, x_lo, y), band: 4 (over x_hi, core).
Axes of the slice: x: 4 (x_hi: 2, x_lo: 2; x = x_hi * 2 + x_lo), y: 4, z: 8, core: 2. Of those that a mesh axis runs over, the one named last changes fastest.
Arguments:
- alpha: bfloat16 [128, 4, 320, 720], P('mem', None, 'band'), may hold values from -6 to 6
- static_ctl: bfloat16 [4, 320, 720], P(None, 'band'), may hold values from -6 to 6
- perturbations: bfloat16 [128, 4, 320, 720], P('mem', None, None, 'band'), may hold values from -16 to 16
- static_std: float32 [4, 320, 720], P(None, None, 'band'), may hold values from 0.5 to 2
- lon_root: bfloat16 [720, 720], replicated, may hold values from -0.11 to 1.11
- lat_root: bfloat16 [320, 320], replicated, may hold values from -0.11 to 1.11
- jacobian: bfloat16 [32, 4, 320, 720], P(None, None, 'mem', 'band'), may hold values from -3 to 3
- obs_count: int32 [320, 720], P('mem', 'band'), may hold values from 1 to 6
- channel_mask: int32 [32, 320, 720], P(None, 'mem', 'band'), may hold values 0 or 1
- channel_error: float32 [32], replicated, may hold values from 1 to 2
- member_weight: int32 [128], replicated, may hold values from 1 to 4
Outputs:
- grad_alpha: float32 [128, 4, 320, 720], P('mem', None, 'band')
- grad_static: float32 [4, 320, 720], P(None, 'band')
All inputs are finite; a program needn't handle non-finite values. No bound on the sum of `channel_mask` on one device may be relied on, other than what follows from the above.
Results may differ from a plain program's by a relative error of at most 0.0055.
Values may be sent and summed in bfloat16 or wider, within the bound.
A program may use at most 64 MiB of HBM per device.

v0:
```python
import jax
import jax.numpy as jnp
from jax import lax
from jax.sharding import PartitionSpec as P


def in_blocks(x, dim, devices):
    lengths = x.shape
    pieces = x.reshape(*lengths[:dim], devices, lengths[dim] // devices, *lengths[dim + 1 :])
    return jnp.moveaxis(pieces, dim, 0)


def sum_at_owner(x, axis, dim):
    pieces = in_blocks(x, dim, lax.axis_size(axis))
    arrived = lax.all_to_all(pieces, axis, split_axis=0, concat_axis=0, tiled=True)
    return arrived.sum(axis=0)


def laid_out(pieces, dim):
    lengths = list(pieces.shape[1:])
    lengths[dim] *= pieces.shape[0]
    return jnp.moveaxis(pieces, 0, dim).reshape(lengths)


def from_everyone(x, axis):
    devices = lax.axis_size(axis)
    return lax.all_to_all(jnp.broadcast_to(x[None], (devices, *x.shape)), axis, 0, 0, tiled=True)


def collect(x, axis, dim):
    return laid_out(from_everyone(x, axis), dim)


def shards(
    alpha,
    static_ctl,
    perturbations,
    static_std,
    lon_root,
    lat_root,
    jacobian,
    obs_count,
    channel_mask,
    channel_error,
    member_weight,
):
    members = alpha.shape[0]
    rows = jacobian.shape[2]
    rank = lax.axis_index("mem")
    weights = member_weight.astype(jnp.float32)
    coef = weights / jnp.sqrt(jnp.sum(weights * weights))
    own_coef = lax.dynamic_slice_in_dim(coef, rank * members, members, 0)
    fields = jnp.concatenate([alpha, static_ctl[None]], axis=0)
    along_lon = jnp.dot(fields, lon_root, preferred_element_type=jnp.float32).astype(jnp.bfloat16)
    regrouped = lax.all_to_all(along_lon, "band", split_axis=3, concat_axis=2, tiled=True)
    along_lat = jnp.einsum("ij,msjk->msik", lat_root, regrouped, preferred_element_type=jnp.float32)
    member_lat = along_lat[:members]
    own_static = lax.dynamic_slice_in_dim(along_lat[members], rank * rows, rows, 1)
    scaled = 0.8 * own_coef
    ensemble_term = jnp.sum(
        scaled[:, None, None, None] * perturbations.astype(jnp.float32) * member_lat, axis=0
    )
    own_sum = sum_at_owner(ensemble_term, "mem", 1)
    own_std = lax.dynamic_slice_in_dim(static_std, rank * rows, rows, 1)
    increment = own_sum + 0.6 * own_std * own_static
    obs_weight = (
        channel_mask.astype(jnp.float32)
        * obs_count.astype(jnp.float32)[None]
        / (channel_error * channel_error)[:, None, None]
    )
    jac_full = jacobian.astype(jnp.float32)
    radiance = jnp.sum(jac_full * increment[None], axis=1)
    obs_gradient = jnp.sum(jac_full * (obs_weight * radiance)[:, None], axis=0).astype(jnp.bfloat16)
    band_gradient = collect(obs_gradient, "mem", 1).astype(jnp.float32)
    member_adjoint = (
        scaled[:, None, None, None] * perturbations.astype(jnp.float32) * band_gradient[None]
    ).astype(jnp.bfloat16)
    static_adjoint = (0.6 * static_std * band_gradient).astype(jnp.bfloat16)
    adjoints = jnp.concatenate([member_adjoint, static_adjoint[None]], axis=0)
    back_lat = jnp.einsum(
        "ji,msjk->msik", lat_root, adjoints, preferred_element_type=jnp.float32
    ).astype(jnp.bfloat16)
    returned = lax.all_to_all(back_lat, "band", split_axis=2, concat_axis=3, tiled=True)
    back_lon = jnp.einsum("msil,jl->msij", returned, lon_root, preferred_element_type=jnp.float32)
    grad_alpha = alpha.astype(jnp.float32) + back_lon[:members]
    grad_static = static_ctl.astype(jnp.float32) + back_lon[members]
    return (grad_alpha, grad_static)


def solution(mesh):
    in_specs = (
        P("mem", None, "band", None),
        P(None, "band", None),
        P("mem", None, None, "band"),
        P(None, None, "band"),
        P(),
        P(),
        P(None, None, "mem", "band"),
        P("mem", "band"),
        P(None, "mem", "band"),
        P(),
        P(),
    )
    out_specs = (P("mem", None, "band", None), P(None, "band", None))
    return jax.shard_map(shards, mesh=mesh, in_specs=in_specs, out_specs=out_specs, check_vma=False)
```

profile of v0, /device:TPU:1, one launch (start us, length us, event | category | flops | bytes accessed | tf_op | source)
XLA Modules:
  0.0 176.1 jit_solution(13423768554717504345)
XLA Ops:
  0.6 1.2 copy-done
  1.9 2.7 %convolution_convert_fusion.1 = bf16[3,4,80,720]{3,2,1,0:T(8,128)(2,1)S(1)} fusion(bf16[1,4,80,720]{3,2,1,0:T(8,128)(2,1)} %bitcast.49, bf16[2,4,80,720]{3,2,1,0:T(8,128)(2,1)} %param.11, bf16[720,720]{1,0:T(8,128)(2,1)S(1)} %copy-done), kind=kOutput, calls=%fused_computation.10 | convolution fusion | flops 996710400 | bytes 3801600 | tf_op jit(solution)/shard_map/dot_general | solution.py:54
  4.6 3.2 %copy.32 = bf16[3,4,80,720]{2,1,0,3:T(4,128)(2,1)} copy(bf16[3,4,80,720]{3,2,1,0:T(8,128)(2,1)S(1)} %convolution_convert_fusion.1) | data formatting | bytes 2764800 | tf_op jit(solution)/shard_map/convert_element_type | solution.py:54
  7.8 7.0 %all-to-all-start = ((bf16[3,4,80,720]{2,1,0,3:T(4,128)(2,1)}), bf16[3,4,80,720]{2,1,0,3:T(4,128)(2,1)S(1)}, u32[]{:S(2)}, u32[]{:S(2)}) async-start(bf16[3,4,80,720]{2,1,0,3:T(4,128)(2,1)} %copy.32), calls=%async_computation | async-start | bytes 4423680 | tf_op jit(solution)/shard_map/all_to_all | solution.py:55
  16.2 26.2 %all-to-all-done = bf16[3,4,80,720]{2,1,0,3:T(4,128)(2,1)S(1)} async-done(((bf16[3,4,80,720]{2,1,0,3:T(4,128)(2,1)}), bf16[3,4,80,720]{2,1,0,3:T(4,128)(2,1)S(1)}, u32[]{:S(2)}, u32[]{:S(2)}) %all-to-all-start) | async-done | bytes 1382432 | tf_op jit(solution)/shard_map/all_to_all | solution.py:55
  42.3 3.8 %copy.33 = bf16[3,4,80,4,180]{4,2,3,1,0:T(8,128)(2,1)} copy(bf16[3,4,80,4,180]{2,1,0,4,3:T(4,128)(2,1)S(1)} %bitcast.44) | data formatting | bytes 2764800 | tf_op jit(solution)/shard_map/all_to_all | solution.py:55
  46.1 3.3 %convolution_bitcast_fusion = f32[3,4,320,180]{2,3,1,0:T(8,128)S(1)} fusion(bf16[3,4,320,180]{3,2,1,0:T(8,128)(2,1)} %bitcast.46, bf16[320,320]{1,0:T(8,128)(2,1)} %param.16), kind=kOutput, calls=%fused_computation.5 | convolution fusion | flops 442368000 | bytes 4352000 | tf_op jit(solution)/shard_map/ij,msjk->msik/dot_general | solution.py:56
  49.4 1.7 copy-done.1
  51.5 1.5 copy.35
  53.0 11.1 %all-to-all-start.1 = ((f32[64,4,5,180]{3,1,2,0:T(4,128)}), f32[64,4,5,180]{3,1,2,0:T(4,128)S(1)}, u32[]{:S(2)}, u32[]{:S(2)}) async-start(f32[64,4,5,180]{3,1,2,0:T(4,128)} %bitcast.47), calls=%async_computation.1 | async-start | bytes 2621440 | tf_op jit(solution)/shard_map/all_to_all | solution.py:15
  64.7 2.1 %constant_dynamic-slice_fusion.1 = f32[4,5,180]{1,0,2:T(4,128)} fusion(f32[4,320,180]{1,0,2:T(4,128)} %param.14, s32[]{:T(128)S(6)} %select_n.8), kind=kLoop, calls=%fused_computation.38 | loop fusion | bytes 28804 | tf_op jit(solution)/shard_map/dynamic_slice | solution.py:64
  66.8 1.9 %copy.47 = f32[4,5,180]{2,0,1:T(4,128)} copy(f32[4,5,180]{1,0,2:T(4,128)} %constant_dynamic-slice_fusion.1) | data formatting | bytes 28800
  69.6 1.2 copy.37
  70.8 24.6 %all-to-all-done.1 = f32[64,4,5,180]{3,1,2,0:T(4,128)S(1)} async-done(((f32[64,4,5,180]{3,1,2,0:T(4,128)}), f32[64,4,5,180]{3,1,2,0:T(4,128)S(1)}, u32[]{:S(2)}, u32[]{:S(2)}) %all-to-all-start.1) | async-done | bytes 921632 | tf_op jit(solution)/shard_map/all_to_all | solution.py:15
  96.7 24.1 %all_to_all.46 = bf16[64,4,5,180]{3,1,2,0:T(4,128)(2,1)S(1)} all-to-all(bf16[64,4,5,180]{3,1,2,0:T(4,128)(2,1)S(1)} %broadcast_in_dim.7), channel_id=1, replica_groups=mesh['mem'=64,'band'=4] {'mem'}, dimensions={0} | all-to-all | bytes 921600 | tf_op jit(solution)/shard_map/all_to_all | solution.py:27
  121.9 1.5 fusion.18
  124.4 2.5 %fusion.4 = bf16[3,4,320,180]{2,3,1,0:T(8,128)(2,1)} fusion(bf16[1,4,320,180]{2,3,1,0:T(8,128)(2,1)S(1)} %fusion.18, bf16[2,4,320,180]{2,3,1,0:T(8,128)(2,1)S(1)} %multiply_convert_fusion, bf16[320,320]{1,0:T(8,128)(2,1)S(1)} %copy-done.7), kind=kOutput, calls=%fused_computation.11 | convolution fusion | flops 443750400 | bytes 2969600 | tf_op jit(solution)/shard_map/ji,msjk->msik/dot_general | solution.py:80
  127.0 6.7 %copy.41 = bf16[3,4,320,180]{3,1,0,2:T(4,128)(2,1)S(1)} copy(bf16[3,4,320,180]{2,3,1,0:T(8,128)(2,1)} %fusion.4) | data formatting | bytes 2764800 | tf_op jit(solution)/shard_map/convert_element_type | solution.py:82
  133.7 32.7 %all_to_all.47 = bf16[3,4,320,180]{3,1,0,2:T(4,128)(2,1)S(1)} all-to-all(bf16[3,4,320,180]{3,1,0,2:T(4,128)(2,1)S(1)} %copy.41), channel_id=1, replica_groups=mesh['mem'=64,'band'=4] {'band'}, dimensions={2} | all-to-all | bytes 2764800 | tf_op jit(solution)/shard_map/all_to_all | solution.py:83
  166.7 1.0 copy.43
  167.7 2.5 %all_to_all.41 = bf16[3,4,80,720]{3,2,1,0:T(8,128)(2,1)} reshape(bf16[3,4,80,4,180]{4,3,2,1,0:T(4,128)(2,1)S(1)} %copy.43) | data formatting | bytes 2764800 | tf_op jit(solution)/shard_map/all_to_all | solution.py:83
  170.2 2.8 %fusion.12 = f32[3,4,80,720]{3,2,1,0:T(8,128)S(1)} fusion(bf16[3,4,80,720]{3,2,1,0:T(8,128)(2,1)} %all_to_all.41, bf16[720,720]{1,0:T(8,128)(2,1)S(1)} %copy-done), kind=kOutput, calls=%fused_computation.18 | convolution fusion | flops 995328000 | bytes 5184000 | tf_op jit(solution)/shard_map/msil,jl->msij/dot_general | solution.py:84
  173.0 1.0 fusion.15
  174.6 1.5 slice_add_fusion
  (49 shorter events, 6.7 us)
Async XLA Ops:
  0.6 1.3 copy-start
  7.8 7.0 %copy-start.14 = (s32[128]{0:T(128)S(1)}, s32[128]{0:T(128)}, u32[]{:S(2)}) copy-start(s32[128]{0:T(128)} %param.21) | copy-start | bytes 1540
  7.8 34.5 %all-to-all-start = ((bf16[3,4,80,720]{2,1,0,3:T(4,128)(2,1)}), bf16[3,4,80,720]{2,1,0,3:T(4,128)(2,1)S(1)}, u32[]{:S(2)}, u32[]{:S(2)}) async-start(bf16[3,4,80,720]{2,1,0,3:T(4,128)(2,1)} %copy.32), calls=%async_computation | async-start | bytes 4423680 | tf_op jit(solution)/shard_map/all_to_all | solution.py:55
  16.1 33.2 %copy-start.11 = (f32[2]{0:T(128)}, f32[2]{0:T(128)S(1)}, u32[]{:S(2)}) copy-start(f32[2]{0:T(128)S(1)} %dynamic-slice_multiply_fusion) | copy-start | bytes 28
  46.1 5.0 %copy-start.2 = (bf16[2,4,320,180]{2,1,3,0:T(4,128)(2,1)S(1)}, bf16[2,4,320,180]{2,1,3,0:T(4,128)(2,1)}, u32[]{:S(2)}) copy-start(bf16[2,4,320,180]{2,1,3,0:T(4,128)(2,1)} %param.13) | copy-start | bytes 2764804
  49.4 1.7 copy-start.1
  53.0 11.2 %copy-start.15 = (f32[32]{0:T(128)S(1)}, f32[32]{0:T(128)}, u32[]{:S(2)}) copy-start(f32[32]{0:T(128)} %param.20) | copy-start | bytes 388
  53.0 11.7 %copy-start.10 = (s32[5,180]{1,0:T(8,128)S(1)}, s32[5,180]{1,0:T(8,128)}, u32[]{:S(2)}) copy-start(s32[5,180]{1,0:T(8,128)} %param.18) | copy-start | bytes 10804
  53.0 42.4 %all-to-all-start.1 = ((f32[64,4,5,180]{3,1,2,0:T(4,128)}), f32[64,4,5,180]{3,1,2,0:T(4,128)S(1)}, u32[]{:S(2)}, u32[]{:S(2)}) async-start(f32[64,4,5,180]{3,1,2,0:T(4,128)} %bitcast.47), calls=%async_computation.1 | async-start | bytes 2621440 | tf_op jit(solution)/shard_map/all_to_all | solution.py:15
  66.8 1.9 %slice-start = ((f32[3,4,320,180]{2,3,1,0:T(8,128)}), f32[1,4,320,180]{2,3,1,0:T(8,128)S(1)}, s32[]{:S(2)}) async-start(f32[3,4,320,180]{2,3,1,0:T(8,128)} %copy-done.1), calls=%async_computation.4 | async-start | bytes 2260992 | tf_op jit(solution)/shard_map/slice | solution.py:58
  69.6 26.1 %copy-start.9 = (f32[4,5,180]{2,0,1:T(4,128)S(1)}, f32[4,5,180]{2,0,1:T(4,128)}, u32[]{:S(2)}) copy-start(f32[4,5,180]{2,0,1:T(4,128)} %copy.47) | copy-start | bytes 43204
  69.6 26.1 %copy-start.4 = (bf16[32,4,5,180]{3,1,2,0:T(4,128)(2,1)S(1)}, bf16[32,4,5,180]{3,1,2,0:T(4,128)(2,1)}, u32[]{:S(2)}) copy-start(bf16[32,4,5,180]{3,1,2,0:T(4,128)(2,1)} %param.17) | copy-start | bytes 691204
  69.6 26.6 %copy-start.8 = (s32[32,5,180]{2,0,1:T(8,128)S(1)}, s32[32,5,180]{2,0,1:T(8,128)}, u32[]{:S(2)}) copy-start(s32[32,5,180]{2,0,1:T(8,128)} %param.19) | copy-start | bytes 345604
  69.6 26.6 %copy-start.13 = (f32[32]{0:T(128)S(1)}, f32[32]{0:T(128)}, u32[]{:S(2)}) copy-start(f32[32]{0:T(128)} %mul.91) | copy-start | bytes 388
  121.9 1.6 copy-start.3
  121.9 1.6 copy-start.12
  123.5 0.9 copy-start.7
  170.2 2.8 %copy-start.6 = (bf16[4,80,720]{2,1,0:T(8,128)(2,1)S(1)}, bf16[4,80,720]{2,1,0:T(8,128)(2,1)}, u32[]{:S(2)}) copy-start(bf16[4,80,720]{2,1,0:T(8,128)(2,1)} %param.12) | copy-start | bytes 1382404
  173.0 1.6 copy-start.5
where the time goes:
time: 177 us; the launch traced here: 176 us
  blocking collectives  56.8 us (32%)
  waiting for transfers between devices  50.7 us (29%)
  local copies, waits for them, and re-layouts  30.3 us (17%)
  starting transfers between devices  18.1 us (10%)
  matrix products  11.2 us (6%)
  other arithmetic  7.28 us (4%)
    all_to_all x1, blocking collectives, shards(): lax.all_to_all(back_lat, 'band', split_axis=2, concat_axis=3, tiled=True)  32.7 us
    all_to_all x1, waiting for transfers between devices, shards(): lax.all_to_all(along_lon, 'band', split_axis=3, concat_axis=2, tiled=True)  26.2 us
    all_to_all x1, waiting for transfers between devices, sum_at_owner(): lax.all_to_all(pieces, axis, split_axis=0, concat_axis=0, tiled=True)  24.6 us
    all_to_all x1, blocking collectives, from_everyone(): lax.all_to_all(jnp.broadcast_to(x[None], (devices, *x.shape)), axis, 0, 0...  24.1 us
    all_to_all x1, starting transfers between devices, sum_at_owner(): lax.all_to_all(pieces, axis, split_axis=0, concat_axis=0, tiled=True)  11.1 us
    all_to_all x1, starting transfers between devices, shards(): lax.all_to_all(along_lon, 'band', split_axis=3, concat_axis=2, tiled=True)  6.96 us
    convert_element_type x1, local copies, waits for them, and re-layouts, shards(): back_lat = jnp.einsum('ji,msjk->msik', lat_root, adjoints, preferred_elem...  6.66 us
    unnamed x33, local copies, waits for them, and re-layouts  5.99 us
  transfers between devices with their start and end apart: 2, of which 2 were waited for; matrix products, arithmetic and copies ran while one was open for 4% of the time, Pallas kernels for 0%

commit v1 on v0

--- a/solution.py
+++ b/solution.py
@@ -52,7 +52,12 @@
     own_coef = lax.dynamic_slice_in_dim(coef, rank * members, members, 0)
     fields = jnp.concatenate([alpha, static_ctl[None]], axis=0)
     along_lon = jnp.dot(fields, lon_root, preferred_element_type=jnp.float32).astype(jnp.bfloat16)
-    regrouped = lax.all_to_all(along_lon, "band", split_axis=3, concat_axis=2, tiled=True)
+    regrouped = jnp.concatenate(
+        lax.all_to_all(
+            jnp.stack(jnp.split(along_lon, lax.axis_size("band"), axis=3)), "band", 0, 0
+        ),
+        axis=2,
+    )
     along_lat = jnp.einsum("ij,msjk->msik", lat_root, regrouped, preferred_element_type=jnp.float32)
     member_lat = along_lat[:members]
     own_static = lax.dynamic_slice_in_dim(along_lat[members], rank * rows, rows, 1)

time: 177 us -> 169 us (0.955)
  local copies, waits for them, and re-layouts: 30.3 us -> 24.9 us
  waiting for transfers between devices: 50.7 us -> 48.1 us
  other arithmetic: 7.28 us -> 9.1 us
    all_to_all x1 -> x0, local copies, waits for them, and re-layouts: 3.75 us -> none  [shards(): lax.all_to_all(along_lon, 'band', split_axis=3, concat_axis=2, tiled=True)]
    convert_element_type x1 -> x0, local copies, waits for them, and re-layouts: 3.25 us -> none  [shards(): jnp.dot(fields, lon_root, preferred_element_type=jnp.float32)]
    all_to_all x1, waiting for transfers between devices: 26.2 us -> 23.5 us  [shards(): lax.all_to_all(jnp.stack(jnp.split(along_lon, lax.axis_size('band'), axis...]
    unnamed x33 -> x35, local copies, waits for them, and re-layouts: 5.99 us -> 6.62 us
where the time goes in v1:
time: 169 us; the launch traced here: 168 us
  blocking collectives  56.8 us (34%)
  waiting for transfers between devices  48.1 us (28%)
  local copies, waits for them, and re-layouts  24.9 us (15%)
  starting transfers between devices  18.1 us (11%)
  matrix products  9.62 us (6%)
  other arithmetic  9.1 us (5%)
    all_to_all x1, blocking collectives, shards(): lax.all_to_all(back_lat, 'band', split_axis=2, concat_axis=3, tiled=True)  32.7 us
    all_to_all x1, waiting for transfers between devices, sum_at_owner(): lax.all_to_all(pieces, axis, split_axis=0, concat_axis=0, tiled=True)  24.5 us
    all_to_all x1, blocking collectives, from_everyone(): lax.all_to_all(jnp.broadcast_to(x[None], (devices, *x.shape)), axis, 0, 0...  24.1 us
    all_to_all x1, waiting for transfers between devices, shards(): lax.all_to_all(jnp.stack(jnp.split(along_lon, lax.axis_size('band'), axis...  23.5 us
    all_to_all x1, starting transfers between devices, sum_at_owner(): lax.all_to_all(pieces, axis, split_axis=0, concat_axis=0, tiled=True)  11.1 us
    all_to_all x1, starting transfers between devices, shards(): lax.all_to_all(jnp.stack(jnp.split(along_lon, lax.axis_size('band'), axis...  6.94 us
    convert_element_type x1, local copies, waits for them, and re-layouts, shards(): back_lat = jnp.einsum('ji,msjk->msik', lat_root, adjoints, preferred_elem...  6.66 us
    unnamed x35, local copies, waits for them, and re-layouts  6.62 us
  transfers between devices with their start and end apart: 2, of which 2 were waited for; matrix products, arithmetic and copies ran while one was open for 4% of the time, Pallas kernels for 0%

profile of v1, /device:TPU:1, one launch (start us, length us, event | category | flops | bytes accessed | tf_op | source)
XLA Modules:
  0.0 168.2 jit_solution(15087523644420518520)
XLA Ops:
  0.6 1.2 copy-done
  1.9 2.7 %convolution_convert_fusion.1 = bf16[3,4,80,720]{3,2,1,0:T(8,128)(2,1)S(1)} fusion(bf16[1,4,80,720]{3,2,1,0:T(8,128)(2,1)} %bitcast.55, bf16[2,4,80,720]{3,2,1,0:T(8,128)(2,1)} %param.11, bf16[720,720]{1,0:T(8,128)(2,1)S(1)} %copy-done), kind=kOutput, calls=%fused_computation.11 | convolution fusion | flops 996710400 | bytes 3801600 | tf_op jit(solution)/shard_map/dot_general | solution.py:54
  5.2 1.8 %pad_maximum_fusion = bf16[4,3,4,80,180]{4,3,2,1,0:T(8,128)(2,1)} fusion(bf16[1,3,4,80,180]{4,3,2,1,0:T(8,128)(2,1)S(1)} %get-tuple-element.3, bf16[1,3,4,80,180]{4,3,2,1,0:T(8,128)(2,1)S(1)} %get-tuple-element.4, bf16[1,3,4,80,180]{4,3,2,1,0:T(8,128)(2,1)S(1)} %get-tuple-element.5, bf16[1,3,4,80,180]{4,3,2,1,0:T(8,128)(2,1)S(1)} %get-tuple-element.2), kind=kLoop, calls=%fused_computation.5 | loop fusion | flops 2073600 | bytes 2764800 | tf_op jit(solution)/shard_map/stack | solution.py:57
  7.0 6.9 %all-to-all-start = ((bf16[4,3,4,80,180]{4,3,2,1,0:T(8,128)(2,1)}), bf16[4,3,4,80,180]{4,3,2,1,0:T(8,128)(2,1)S(1)}, u32[]{:S(2)}, u32[]{:S(2)}) async-start(bf16[4,3,4,80,180]{4,3,2,1,0:T(8,128)(2,1)} %pad_maximum_fusion), calls=%async_computation | async-start | bytes 3932160 | tf_op jit(solution)/shard_map/all_to_all | solution.py:56
  15.3 23.5 %all-to-all-done = bf16[4,3,4,80,180]{4,3,2,1,0:T(8,128)(2,1)S(1)} async-done(((bf16[4,3,4,80,180]{4,3,2,1,0:T(8,128)(2,1)}), bf16[4,3,4,80,180]{4,3,2,1,0:T(8,128)(2,1)S(1)}, u32[]{:S(2)}, u32[]{:S(2)}) %all-to-all-start) | async-done | bytes 1382432 | tf_op jit(solution)/shard_map/all_to_all | solution.py:56
  39.8 1.6 convolution_bitcast_fusion
  41.5 1.7 %copy-done.1 = f32[3,4,320,180]{2,3,1,0:T(8,128)} copy-done((f32[3,4,320,180]{2,3,1,0:T(8,128)}, f32[3,4,320,180]{2,3,1,0:T(8,128)S(1)}, u32[]{:S(2)}) %copy-start.1) | copy-done | bytes 2764824
  43.6 1.5 copy.33
  45.1 11.1 %all-to-all-start.1 = ((f32[64,4,5,180]{3,1,2,0:T(4,128)}), f32[64,4,5,180]{3,1,2,0:T(4,128)S(1)}, u32[]{:S(2)}, u32[]{:S(2)}) async-start(f32[64,4,5,180]{3,1,2,0:T(4,128)} %bitcast.53), calls=%async_computation.1 | async-start | bytes 2621440 | tf_op jit(solution)/shard_map/all_to_all | solution.py:15
  56.8 2.2 %constant_dynamic-slice_fusion.1 = f32[4,5,180]{1,0,2:T(4,128)} fusion(f32[4,320,180]{1,0,2:T(4,128)} %param.14, s32[]{:T(128)S(6)} %select_n.8), kind=kLoop, calls=%fused_computation.43 | loop fusion | bytes 28804 | tf_op jit(solution)/shard_map/dynamic_slice | solution.py:69
  59.0 1.8 %copy.45 = f32[4,5,180]{2,0,1:T(4,128)} copy(f32[4,5,180]{1,0,2:T(4,128)} %constant_dynamic-slice_fusion.1) | data formatting | bytes 28800
  61.7 1.2 copy.35
  63.0 24.5 %all-to-all-done.1 = f32[64,4,5,180]{3,1,2,0:T(4,128)S(1)} async-done(((f32[64,4,5,180]{3,1,2,0:T(4,128)}), f32[64,4,5,180]{3,1,2,0:T(4,128)S(1)}, u32[]{:S(2)}, u32[]{:S(2)}) %all-to-all-start.1) | async-done | bytes 921632 | tf_op jit(solution)/shard_map/all_to_all | solution.py:15
  88.8 24.1 %all_to_all.33 = bf16[64,4,5,180]{3,1,2,0:T(4,128)(2,1)S(1)} all-to-all(bf16[64,4,5,180]{3,1,2,0:T(4,128)(2,1)S(1)} %broadcast_in_dim.7), channel_id=1, replica_groups=mesh['mem'=64,'band'=4] {'mem'}, dimensions={0} | all-to-all | bytes 921600 | tf_op jit(solution)/shard_map/all_to_all | solution.py:27
  113.1 0.9 copy.36
  114.0 1.5 fusion.18
  116.5 2.5 %fusion.4 = bf16[3,4,320,180]{2,3,1,0:T(8,128)(2,1)} fusion(bf16[1,4,320,180]{2,3,1,0:T(8,128)(2,1)S(1)} %fusion.18, bf16[2,4,320,180]{2,3,1,0:T(8,128)(2,1)S(1)} %multiply_convert_fusion, bf16[320,320]{1,0:T(8,128)(2,1)S(1)} %copy-done.8), kind=kOutput, calls=%fused_computation.12 | convolution fusion | flops 443750400 | bytes 2969600 | tf_op jit(solution)/shard_map/ji,msjk->msik/dot_general | solution.py:85
  119.1 6.7 %copy.39 = bf16[3,4,320,180]{3,1,0,2:T(4,128)(2,1)S(1)} copy(bf16[3,4,320,180]{2,3,1,0:T(8,128)(2,1)} %fusion.4) | data formatting | bytes 2764800 | tf_op jit(solution)/shard_map/convert_element_type | solution.py:87
  125.7 32.7 %all_to_all.34 = bf16[3,4,320,180]{3,1,0,2:T(4,128)(2,1)S(1)} all-to-all(bf16[3,4,320,180]{3,1,0,2:T(4,128)(2,1)S(1)} %copy.39), channel_id=1, replica_groups=mesh['mem'=64,'band'=4] {'band'}, dimensions={2} | all-to-all | bytes 2764800 | tf_op jit(solution)/shard_map/all_to_all | solution.py:88
  158.8 1.0 copy.41
  159.8 2.5 %all_to_all.28 = bf16[3,4,80,720]{3,2,1,0:T(8,128)(2,1)} reshape(bf16[3,4,80,4,180]{4,3,2,1,0:T(4,128)(2,1)S(1)} %copy.41) | data formatting | bytes 2764800 | tf_op jit(solution)/shard_map/all_to_all | solution.py:88
  162.3 2.8 %fusion.12 = f32[3,4,80,720]{3,2,1,0:T(8,128)S(1)} fusion(bf16[3,4,80,720]{3,2,1,0:T(8,128)(2,1)} %all_to_all.28, bf16[720,720]{1,0:T(8,128)(2,1)S(1)} %copy-done), kind=kOutput, calls=%fused_computation.19 | convolution fusion | flops 995328000 | bytes 5184000 | tf_op jit(solution)/shard_map/msil,jl->msij/dot_general | solution.py:89
  165.1 1.0 fusion.15
  166.7 1.5 slice_add_fusion
  (52 shorter events, 7.4 us)
Async XLA Ops:
  0.6 1.3 copy-start
  7.0 6.9 %copy-start.15 = (s32[128]{0:T(128)S(1)}, s32[128]{0:T(128)}, u32[]{:S(2)}) copy-start(s32[128]{0:T(128)} %param.21) | copy-start | bytes 1540
  7.0 31.9 %all-to-all-start = ((bf16[4,3,4,80,180]{4,3,2,1,0:T(8,128)(2,1)}), bf16[4,3,4,80,180]{4,3,2,1,0:T(8,128)(2,1)S(1)}, u32[]{:S(2)}, u32[]{:S(2)}) async-start(bf16[4,3,4,80,180]{4,3,2,1,0:T(8,128)(2,1)} %pad_maximum_fusion), calls=%async_computation | async-start | bytes 3932160 | tf_op jit(solution)/shard_map/all_to_all | solution.py:56
  15.3 26.1 %copy-start.12 = (f32[2]{0:T(128)}, f32[2]{0:T(128)S(1)}, u32[]{:S(2)}) copy-start(f32[2]{0:T(128)S(1)} %dynamic-slice_multiply_fusion) | copy-start | bytes 28
  38.9 0.9 copy-start.7
  39.8 3.4 %copy-start.2 = (bf16[2,4,320,180]{2,1,3,0:T(4,128)(2,1)S(1)}, bf16[2,4,320,180]{2,1,3,0:T(4,128)(2,1)}, u32[]{:S(2)}) copy-start(bf16[2,4,320,180]{2,1,3,0:T(4,128)(2,1)} %param.13) | copy-start | bytes 2764804
  41.5 1.7 %copy-start.1 = (f32[3,4,320,180]{2,3,1,0:T(8,128)}, f32[3,4,320,180]{2,3,1,0:T(8,128)S(1)}, u32[]{:S(2)}) copy-start(f32[3,4,320,180]{2,3,1,0:T(8,128)S(1)} %convolution_bitcast_fusion) | copy-start | bytes 8294404
  45.1 11.2 %copy-start.16 = (f32[32]{0:T(128)S(1)}, f32[32]{0:T(128)}, u32[]{:S(2)}) copy-start(f32[32]{0:T(128)} %param.20) | copy-start | bytes 388
  45.1 11.7 %copy-start.11 = (s32[5,180]{1,0:T(8,128)S(1)}, s32[5,180]{1,0:T(8,128)}, u32[]{:S(2)}) copy-start(s32[5,180]{1,0:T(8,128)} %param.18) | copy-start | bytes 10804
  45.1 42.4 %all-to-all-start.1 = ((f32[64,4,5,180]{3,1,2,0:T(4,128)}), f32[64,4,5,180]{3,1,2,0:T(4,128)S(1)}, u32[]{:S(2)}, u32[]{:S(2)}) async-start(f32[64,4,5,180]{3,1,2,0:T(4,128)} %bitcast.53), calls=%async_computation.1 | async-start | bytes 2621440 | tf_op jit(solution)/shard_map/all_to_all | solution.py:15
  56.8 4.0 %slice-start = ((f32[3,4,320,180]{2,3,1,0:T(8,128)}), f32[1,4,320,180]{2,3,1,0:T(8,128)S(1)}, s32[]{:S(2)}) async-start(f32[3,4,320,180]{2,3,1,0:T(8,128)} %copy-done.1), calls=%async_computation.4 | async-start | bytes 2260992 | tf_op jit(solution)/shard_map/slice | solution.py:63
  61.7 26.0 %copy-start.10 = (f32[4,5,180]{2,0,1:T(4,128)S(1)}, f32[4,5,180]{2,0,1:T(4,128)}, u32[]{:S(2)}) copy-start(f32[4,5,180]{2,0,1:T(4,128)} %copy.45) | copy-start | bytes 43204
  61.7 26.1 %copy-start.4 = (bf16[32,4,5,180]{3,1,2,0:T(4,128)(2,1)S(1)}, bf16[32,4,5,180]{3,1,2,0:T(4,128)(2,1)}, u32[]{:S(2)}) copy-start(bf16[32,4,5,180]{3,1,2,0:T(4,128)(2,1)} %param.17) | copy-start | bytes 691204
  61.7 26.5 %copy-start.9 = (s32[32,5,180]{2,0,1:T(8,128)S(1)}, s32[32,5,180]{2,0,1:T(8,128)}, u32[]{:S(2)}) copy-start(s32[32,5,180]{2,0,1:T(8,128)} %param.19) | copy-start | bytes 345604
  61.7 26.5 %copy-start.14 = (f32[32]{0:T(128)S(1)}, f32[32]{0:T(128)}, u32[]{:S(2)}) copy-start(f32[32]{0:T(128)} %mul.91) | copy-start | bytes 388
  114.0 1.6 copy-start.3
  114.0 1.6 copy-start.13
  115.6 0.9 copy-start.8
  162.3 2.8 %copy-start.6 = (bf16[4,80,720]{2,1,0:T(8,128)(2,1)S(1)}, bf16[4,80,720]{2,1,0:T(8,128)(2,1)}, u32[]{:S(2)}) copy-start(bf16[4,80,720]{2,1,0:T(8,128)(2,1)} %param.12) | copy-start | bytes 1382404
  165.1 1.6 copy-start.5
